TPU v7x, 32 devices: a whole 2x2x4 slice. The times are simulated.
32 devices in a mesh: parts: 2 (over y), row: 4 (over z), frame: 4 (over x, core).
Axes of the slice: x: 2, y: 2, z: 4, core: 2. Of those that a mesh axis runs over, the one named last changes fastest.
Arguments:
- latent: bfloat16 [8, 8, 16, 512], P(('parts', 'frame'), 'row'), parts along dimension 0, may hold values from -15 to 15
- qkv_weight: bfloat16 [3, 512, 512], P(None, 'frame'), may hold values from -0.125 to 0.125
- out_weight: bfloat16 [512, 512], P('frame'), may hold values from -0.25 to 0.25
- attn_gain: float32 [512], replicated, may hold values from 0.1 to 1.9
- in_weight: bfloat16 [512, 2, 2048], P(None, None, 'frame'), may hold values from -0.25 to 0.25
- depth_weight: float32 [3, 3, 2, 2048], replicated, may hold values from -2 to 2
- down_weight: bfloat16 [2048, 512], P('frame'), may hold values from -0.125 to 0.125
- mlp_gain: float32 [512], replicated, may hold values from 0.1 to 1.9
- conv_first: bfloat16 [3, 3, 3, 512, 512], P(None, None, None, 'frame'), may hold values from -0.0546875 to 0.0546875
- conv_second: bfloat16 [3, 3, 3, 512, 512], P(None, None, None, 'frame'), may hold values from -0.0546875 to 0.0546875
Outputs:
- decoded: bfloat16 [8, 8, 16, 512], P('parts', 'row', 'frame'), parts along dimension 0
There are 2 independent parts, one for each index of `parts`. A program takes and returns all parts, laid end to end along the dimension named above; an argument that names none is the same for every part. Nothing has to cross between parts.
All inputs are finite; a program needn't handle non-finite values.
Results may differ from a plain program's by a relative error of at most 0.015.
Values may be sent and summed in bfloat16 or wider, within the bound.
A program may use at most 128 MiB of HBM per device.

v0:
```python
import jax
import jax.numpy as jnp
from jax import lax
from jax.sharding import PartitionSpec as P

HEAD = 32


def padded_2(cells, sides, width):
    for axis, dim in sides:
        count = lax.axis_size(axis)
        ends = count - 1
        head = lax.slice_in_dim(cells, 0, width, axis=dim)
        tail = lax.slice_in_dim(cells, cells.shape[dim] - width, cells.shape[dim], axis=dim)
        cells = jnp.concatenate(
            [
                lax.ppermute(tail, axis, [(i, (i + 1) % count) for i in range(ends)]),
                cells,
                lax.ppermute(head, axis, [((i + 1) % count, i) for i in range(ends)]),
            ],
            axis=dim,
        )
    return cells


def norm_rows(values, gain):
    return values * lax.rsqrt(jnp.mean(values * values, axis=-1, keepdims=True) + 1e-05) * gain


def attend(packed):
    frames, height, columns = (packed.shape[0], packed.shape[1], packed.shape[2])
    width = packed.shape[4]
    heads = width // HEAD
    flat = packed.reshape(frames, height * columns, 3, heads, HEAD)
    query = jnp.maximum(flat[:, :, 0], 0)
    keys = jnp.maximum(flat[:, :, 1], 0)
    values = flat[:, :, 2]
    state = jnp.einsum("fnhd,fnhe->fhde", keys, values, preferred_element_type=jnp.float32)
    key_total = jnp.sum(keys.astype(jnp.float32), axis=1)
    state, key_total = (
        lax.psum(state.astype(jnp.bfloat16), "row").astype(jnp.float32),
        lax.psum(key_total.astype(jnp.bfloat16), "row").astype(jnp.float32),
    )
    count = height * lax.axis_size("row") * columns
    state = state / count
    key_mean = key_total / count
    query_wide = query.astype(jnp.float32)
    numer = jnp.einsum("fnhd,fhde->fnhe", query_wide, state, precision=lax.Precision.HIGHEST)
    denom = jnp.maximum(
        jnp.einsum("fnhd,fhd->fnh", query_wide, key_mean, precision=lax.Precision.HIGHEST), 1.0
    )
    return (numer / denom[..., None]).astype(jnp.bfloat16).reshape(frames, height, columns, width)


def depth_mix(inner, depth_local):
    height, columns = (inner.shape[1], inner.shape[2])
    extended = padded_2(inner, (("row", 1),), 1)
    padded = jnp.pad(extended, ((0, 0), (0, 0), (1, 1), (0, 0), (0, 0)))
    spread = jnp.zeros(inner.shape, jnp.float32)
    for shift_row in range(3):
        for shift_col in range(3):
            spread = (
                spread
                + padded[:, shift_row : shift_row + height, shift_col : shift_col + columns].astype(
                    jnp.float32
                )
                * depth_local[shift_row, shift_col]
            )
    return (spread[..., 0, :] * jax.nn.silu(spread[..., 1, :])).astype(jnp.bfloat16)


def conv_tile(extended, kernel):
    frames, padded_rows, columns, width = extended.shape
    height = padded_rows - 2
    out_width = kernel.shape[3]
    padded = jnp.pad(extended, ((1, 1), (0, 0), (1, 1), (0, 0)))
    result = jnp.zeros((frames * height * columns, out_width), jnp.float32)
    for shift_time in range(3):
        for shift_row in range(3):
            slab = padded[shift_time : shift_time + frames, shift_row : shift_row + height]
            stacked = jnp.stack(
                [slab[:, :, shift_col : shift_col + columns] for shift_col in range(3)], axis=3
            )
            result = result + jnp.einsum(
                "nci,coi->no",
                stacked.reshape(-1, 3, width),
                kernel[shift_time, shift_row],
                preferred_element_type=jnp.float32,
            )
    return result.reshape(frames, height, columns, out_width)


def local(
    latent,
    qkv_weight,
    out_weight,
    attn_gain,
    in_weight,
    depth_weight,
    down_weight,
    mlp_gain,
    conv_first,
    conv_second,
):
    frames, height, columns, width = latent.shape
    place = lax.axis_index("frame")
    packed = jnp.einsum(
        "frwc,kjc->frwkj",
        latent,
        lax.all_gather(qkv_weight, "frame", axis=1, tiled=True),
        preferred_element_type=jnp.float32,
    ).astype(jnp.bfloat16)
    mixed = attend(packed)
    section = mixed
    attn_out = jnp.einsum(
        "frwj,jc->frwc",
        section,
        lax.all_gather(out_weight, "frame", axis=0, tiled=True),
        preferred_element_type=jnp.float32,
    )
    first = (latent.astype(jnp.float32) + norm_rows(attn_out, attn_gain)).astype(jnp.bfloat16)
    inner = jax.nn.silu(
        jnp.einsum(
            "frwc,ckj->frwkj",
            first,
            lax.all_gather(in_weight, "frame", axis=2, tiled=True),
            preferred_element_type=jnp.float32,
        )
    ).astype(jnp.bfloat16)
    gated = depth_mix(inner, depth_weight)
    section = gated
    mlp_out = jnp.einsum(
        "frwj,jc->frwc",
        section,
        lax.all_gather(down_weight, "frame", axis=0, tiled=True),
        preferred_element_type=jnp.float32,
    )
    second = (first.astype(jnp.float32) + norm_rows(mlp_out, mlp_gain)).astype(jnp.bfloat16)
    gathered = lax.all_gather(second, "frame", axis=0, tiled=True)
    out_share = conv_first.shape[3]
    extended = padded_2(gathered, (("row", 1),), 2)
    activated = jax.nn.silu(conv_tile(extended, conv_first))
    global_row = lax.axis_index("row") * height - 1 + lax.iota(jnp.int32, height + 2)
    inside = ((global_row >= 0) & (global_row < height * lax.axis_size("row"))).astype(jnp.float32)
    hidden_conv = (activated * inside[None, :, None, None]).astype(jnp.bfloat16)
    joined = lax.all_gather(hidden_conv, "frame", axis=3, tiled=True)
    result = conv_tile(joined, conv_second)
    own_part = lax.dynamic_slice_in_dim(gathered, place * out_share, out_share, 3)
    final = (own_part.astype(jnp.float32) + result).astype(jnp.bfloat16)
    return lax.all_to_all(final, "frame", split_axis=2, concat_axis=3, tiled=True)


def solution(mesh):
    in_specs = (
        P(("parts", "frame"), "row", None, None),
        P(None, "frame", None),
        P("frame", None),
        P(),
        P(None, None, "frame"),
        P(),
        P("frame", None),
        P(),
        P(None, None, None, "frame", None),
        P(None, None, None, "frame", None),
    )
    out_specs = P("parts", "row", "frame", None)
    return jax.shard_map(local, mesh=mesh, in_specs=in_specs, out_specs=out_specs, check_vma=False)
```

profile of v0, /device:TPU:0, one launch (start us, length us, event | category | flops | bytes accessed | tf_op | source)
XLA Modules:
  0.0 137.9 jit_solution(649510478248561732)
XLA Ops:
  6.5 0.7 all-gather.4.cloned.1.call-update
  7.3 2.4 %copy.34 = bf16[512,2,512]{2,0,1:T(8,128)(2,1)} copy(bf16[512,2,512]{2,1,0:T(2,128)(2,1)} %param.14) | data formatting | bytes 2097152 | tf_op args[4]
  9.8 0.7 all-gather.8.cloned.1.call-update
  10.5 8.6 %all_gather.19 = bf16[512,512]{1,0:T(8,128)(2,1)S(1)} all-gather(bf16[128,512]{1,0:T(8,128)(2,1)S(1)} %copy-done.1), channel_id=1, replica_groups=mesh['parts'=2,'row'=4,'frame'=4] {'frame'}, dimensions={0}, use_global_device_ids=true | all-gather | bytes 655360 | tf_op jit(solution)/shard_map/all_gather | solution.py:118
  19.1 12.1 %all-gather.4.cloned.1.call-done = bf16[3,512,512]{2,1,0:T(8,128)(2,1)} async-done(((bf16[3,128,512]{2,1,0:T(8,128)(2,1)}), bf16[3,512,512]{2,1,0:T(8,128)(2,1)}) %all-gather.4.cloned.1.call-update) | async-done | bytes 1572880 | tf_op jit(solution)/shard_map/all_gather | solution.py:110
  31.3 2.0 %fusion.7 = bf16[2,16,3,512]{3,1,2,0:T(8,128)(2,1)S(1)} fusion(bf16[3,512,512]{2,1,0:T(8,128)(2,1)} %all-gather.4.cloned.1.call-done, bf16[1,2,16,512]{3,2,1,0:T(8,128)(2,1)S(1)} %copy-done.2), kind=kOutput, calls=%fused_computation.59 | convolution fusion | flops 50380800 | bytes 1703936 | tf_op jit(solution)/shard_map/frwc,kjc->frwkj/dot_general | solution.py:107
  34.0 21.4 %all-reduce.3 = (bf16[1,16,32,32]{3,2,1,0:T(8,128)(2,1)S(1)}, bf16[1,16,32]{2,1,0:T(8,128)(2,1)S(1)}) all-reduce(bf16[1,16,32,32]{3,2,1,0:T(8,128)(2,1)S(1)} %fusion.10, bf16[1,16,32]{2,1,0:T(8,128)(2,1)S(1)} %bitcast.373), channel_id=1, replica_groups=mesh['parts'=2,'row'=4,'frame'=4] {'row'}, use_global_device_ids=true, to_apply=%region_0.0 | all-reduce | flops 16896 | bytes 67584 | tf_op jit(solution)/shard_map/psum | solution.py:41
  57.0 10.4 %all-gather.6.cloned.1.call-done = bf16[512,2,2048]{2,0,1:T(8,128)(2,1)} async-done(((bf16[512,2,512]{2,0,1:T(8,128)(2,1)}), bf16[512,2,2048]{2,0,1:T(8,128)(2,1)}) %all-gather.6.cloned.1.call-update) | async-done | bytes 4194320 | tf_op jit(solution)/shard_map/all_gather | solution.py:126
  67.3 3.0 %multiply_convert_fusion = bf16[2,16,2,2048]{3,1,2,0:T(8,128)(2,1)S(1)} fusion(bf16[512,2,2048]{2,0,1:T(8,128)(2,1)} %all-gather.6.cloned.1.call-done, bf16[1,2,16,512]{3,2,1,0:T(8,128)(2,1)S(1)} %fusion.184), kind=kOutput, calls=%fused_computation.154 | convolution fusion | flops 134873088 | bytes 4489216 | tf_op jit(solution)/shard_map/frwc,ckj->frwkj/dot_general | solution.py:123
  70.4 3.4 %collective-permute-start = (bf16[1,1,16,2,2048]{4,2,3,1,0:T(8,128)(2,1)S(1)}, bf16[1,1,16,2,2048]{4,2,3,1,0:T(8,128)(2,1)S(1)}, u32[]{:S(2)}, u32[]{:S(2)}) collective-permute-start(bf16[1,1,16,2,2048]{4,2,3,1,0:T(8,128)(2,1)S(1)} %get-tuple-element.62), channel_id=1, source_target_pairs={{0,4},{4,8},{8,12},{1,5},{5,9},{9,13},{2,6},{6,10},{10,14},{3,7},{... | collective-permute-start | bytes 393224 | tf_op jit(solution)/shard_map/ppermute | solution.py:17
  73.8 1.3 collective-permute-start.1
  75.1 1.8 %collective-permute-done = bf16[1,1,16,2,2048]{4,2,3,1,0:T(8,128)(2,1)S(1)} collective-permute-done((bf16[1,1,16,2,2048]{4,2,3,1,0:T(8,128)(2,1)S(1)}, bf16[1,1,16,2,2048]{4,2,3,1,0:T(8,128)(2,1)S(1)}, u32[]{:S(2)}, u32[]{:S(2)}) %collective-permute-start) | collective-permute-done | bytes 131104 | tf_op jit(solution)/shard_map/ppermute | solution.py:17
  76.9 4.1 %collective-permute-done.1 = bf16[1,1,16,2,2048]{4,2,3,1,0:T(8,128)(2,1)S(1)} collective-permute-done((bf16[1,1,16,2,2048]{4,2,3,1,0:T(8,128)(2,1)S(1)}, bf16[1,1,16,2,2048]{4,2,3,1,0:T(8,128)(2,1)S(1)}, u32[]{:S(2)}, u32[]{:S(2)}) %collective-permute-start.1) | collective-permute-done | bytes 131104 | tf_op jit(solution)/shard_map/ppermute | solution.py:19
  81.8 9.7 %all-gather.8.cloned.1.call-done = bf16[2048,512]{1,0:T(8,128)(2,1)} async-done(((bf16[512,512]{1,0:T(8,128)(2,1)}), bf16[2048,512]{1,0:T(8,128)(2,1)}) %all-gather.8.cloned.1.call-update) | async-done | bytes 2097168 | tf_op jit(solution)/shard_map/all_gather | solution.py:135
  91.5 2.1 %multiply_reduce_fusion = (f32[2,16]{1,0:T(2,128)S(1)}, f32[2,16,512]{2,1,0:T(8,128)S(1)}) fusion(bf16[2048,512]{1,0:T(8,128)(2,1)} %all-gather.8.cloned.1.call-done, f32[1,2,16,2,2048]{4,2,3,1,0:T(8,128)S(1)} %fusion.82), kind=kOutput, calls=%fused_computation.264 | convolution fusion | flops 67534816 | bytes 2687104 | tf_op jit(solution)/shard_map/frwj,jc->frwc/dot_general | solution.py:132
  93.7 5.4 %all_gather.22 = bf16[4,2,16,512]{3,2,1,0:T(8,128)(2,1)S(1)} all-gather(bf16[1,2,16,512]{3,2,1,0:T(8,128)(2,1)S(1)} %fusion.183), channel_id=1, replica_groups=mesh['parts'=2,'row'=4,'frame'=4] {'frame'}, dimensions={0}, use_global_device_ids=true | all-gather | bytes 163840 | tf_op jit(solution)/shard_map/all_gather | solution.py:139
  99.1 3.4 %collective-permute-start.2 = (bf16[4,2,16,512]{3,2,1,0:T(8,128)(2,1)S(1)}, bf16[4,2,16,512]{3,2,1,0:T(8,128)(2,1)S(1)}, u32[]{:S(2)}, u32[]{:S(2)}) collective-permute-start(bf16[4,2,16,512]{3,2,1,0:T(8,128)(2,1)S(1)} %all_gather.22), channel_id=1, source_target_pairs={{0,4},{4,8},{8,12},{1,5},{5,9},{9,13},{2,6},{6,10},{10,14},{3,7},{... | collective-permute-start | bytes 393224 | tf_op jit(solution)/shard_map/ppermute | solution.py:17
  102.5 1.3 collective-permute-start.3
  103.8 1.9 %collective-permute-done.2 = bf16[4,2,16,512]{3,2,1,0:T(8,128)(2,1)S(1)} collective-permute-done((bf16[4,2,16,512]{3,2,1,0:T(8,128)(2,1)S(1)}, bf16[4,2,16,512]{3,2,1,0:T(8,128)(2,1)S(1)}, u32[]{:S(2)}, u32[]{:S(2)}) %collective-permute-start.2) | collective-permute-done | bytes 131104 | tf_op jit(solution)/shard_map/ppermute | solution.py:17
  105.8 4.1 %collective-permute-done.3 = bf16[4,2,16,512]{3,2,1,0:T(8,128)(2,1)S(1)} collective-permute-done((bf16[4,2,16,512]{3,2,1,0:T(8,128)(2,1)S(1)}, bf16[4,2,16,512]{3,2,1,0:T(8,128)(2,1)S(1)}, u32[]{:S(2)}, u32[]{:S(2)}) %collective-permute-start.3) | collective-permute-done | bytes 131104 | tf_op jit(solution)/shard_map/ppermute | solution.py:19
  109.9 0.8 pad_slice_fusion.23
  110.9 1.0 copy-done.5
  115.4 5.9 %all_gather.23 = bf16[4,4,16,512]{3,2,1,0:T(8,128)(2,1)S(1)} all-gather(bf16[4,4,16,128]{3,2,1,0:T(8,128)(2,1)S(1)} %multiply_convert_fusion.1), channel_id=1, replica_groups=mesh['parts'=2,'row'=4,'frame'=4] {'frame'}, dimensions={3}, use_global_device_ids=true | all-gather | bytes 327680 | tf_op jit(solution)/shard_map/all_gather | solution.py:146
  124.4 6.3 %all_to_all.18 = bf16[4,2,16,128]{3,1,0,2:T(2,128)(2,1)S(1)} all-to-all(bf16[4,2,16,128]{3,1,0,2:T(2,128)(2,1)S(1)} %copy.36), channel_id=1, replica_groups=mesh['parts'=2,'row'=4,'frame'=4] {'frame'}, dimensions={2} | all-to-all | bytes 65536 | tf_op jit(solution)/shard_map/all_to_all | solution.py:150
  (70 shorter events, 10.5 us)
Async XLA Ops:
  6.5 4.0 %copy-start.1 = (bf16[128,512]{1,0:T(8,128)(2,1)S(1)}, bf16[128,512]{1,0:T(8,128)(2,1)}, u32[]{:S(2)}) copy-start(bf16[128,512]{1,0:T(8,128)(2,1)} %param.12) | copy-start | bytes 393220
  6.5 24.7 %copy-start.2 = (bf16[1,2,16,512]{3,2,1,0:T(8,128)(2,1)S(1)}, bf16[1,2,16,512]{3,2,1,0:T(8,128)(2,1)}, u32[]{:S(2)}) copy-start(bf16[1,2,16,512]{3,2,1,0:T(8,128)(2,1)} %param.10) | copy-start | bytes 98308
  6.5 24.7 %all-gather.4.cloned.1.call-start = ((), (), s32[]{:S(2)}) async-start(), calls=%async_computation.1 | async-start | bytes 1966080 | tf_op jit(solution)/shard_map/all_gather | solution.py:110
  7.3 60.1 %all-gather.6.cloned.1.call-start = ((), (), s32[]{:S(2)}) async-start(), calls=%async_computation.2 | async-start | bytes 5242880 | tf_op jit(solution)/shard_map/all_gather | solution.py:126
  9.7 81.7 %all-gather.8.cloned.1.call-start = ((), (), s32[]{:S(2)}) async-start(), calls=%async_computation.3 | async-start | bytes 2621440 | tf_op jit(solution)/shard_map/all_gather | solution.py:135
  19.1 37.7 %copy-start.3 = (f32[512]{0:T(512)S(1)}, f32[512]{0:T(512)}, u32[]{:S(2)}) copy-start(f32[512]{0:T(512)} %param.13) | copy-start | bytes 6148
  56.9 18.2 %copy-start = (f32[3,3,2,2048]{3,2,1,0:T(2,128)S(1)}, f32[3,3,2,2048]{3,2,1,0:T(2,128)}, u32[]{:S(2)}) copy-start(f32[3,3,2,2048]{3,2,1,0:T(2,128)} %param.15) | copy-start | bytes 442372
  70.4 6.5 %collective-permute-start = (bf16[1,1,16,2,2048]{4,2,3,1,0:T(8,128)(2,1)S(1)}, bf16[1,1,16,2,2048]{4,2,3,1,0:T(8,128)(2,1)S(1)}, u32[]{:S(2)}, u32[]{:S(2)}) collective-permute-start(bf16[1,1,16,2,2048]{4,2,3,1,0:T(8,128)(2,1)S(1)} %get-tuple-element.62), channel_id=1, source_target_pairs={{0,4},{4,8},{8,12},{1,5},{5,9},{9,13},{2,6},{6,10},{10,14},{3,7},{... | collective-permute-start | bytes 393224 | tf_op jit(solution)/shard_map/ppermute | solution.py:17
  73.8 7.3 %collective-permute-start.1 = (bf16[1,1,16,2,2048]{4,2,3,1,0:T(8,128)(2,1)S(1)}, bf16[1,1,16,2,2048]{4,2,3,1,0:T(8,128)(2,1)S(1)}, u32[]{:S(2)}, u32[]{:S(2)}) collective-permute-start(bf16[1,1,16,2,2048]{4,2,3,1,0:T(8,128)(2,1)S(1)} %get-tuple-element.63), channel_id=1, source_target_pairs={{4,0},{8,4},{12,8},{5,1},{9,5},{13,9},{6,2},{10,6},{14,10},{7,3},{... | collective-permute-start | bytes 393224 | tf_op jit(solution)/shard_map/ppermute | solution.py:19
  75.1 18.4 %copy-start.4 = (f32[512]{0:T(512)S(1)}, f32[512]{0:T(512)}, u32[]{:S(2)}) copy-start(f32[512]{0:T(512)} %param.17) | copy-start | bytes 6148
  99.1 6.6 %collective-permute-start.2 = (bf16[4,2,16,512]{3,2,1,0:T(8,128)(2,1)S(1)}, bf16[4,2,16,512]{3,2,1,0:T(8,128)(2,1)S(1)}, u32[]{:S(2)}, u32[]{:S(2)}) collective-permute-start(bf16[4,2,16,512]{3,2,1,0:T(8,128)(2,1)S(1)} %all_gather.22), channel_id=1, source_target_pairs={{0,4},{4,8},{8,12},{1,5},{5,9},{9,13},{2,6},{6,10},{10,14},{3,7},{... | collective-permute-start | bytes 393224 | tf_op jit(solution)/shard_map/ppermute | solution.py:17
  102.5 7.4 %collective-permute-start.3 = (bf16[4,2,16,512]{3,2,1,0:T(8,128)(2,1)S(1)}, bf16[4,2,16,512]{3,2,1,0:T(8,128)(2,1)S(1)}, u32[]{:S(2)}, u32[]{:S(2)}) collective-permute-start(bf16[4,2,16,512]{3,2,1,0:T(8,128)(2,1)S(1)} %all_gather.22), channel_id=1, source_target_pairs={{4,0},{8,4},{12,8},{5,1},{9,5},{13,9},{6,2},{10,6},{14,10},{7,3},{... | collective-permute-start | bytes 393224 | tf_op jit(solution)/shard_map/ppermute | solution.py:19
  109.9 2.0 %copy-start.5 = (bf16[3,3,3,128,512]{4,3,2,1,0:T(8,128)(2,1)S(1)}, bf16[3,3,3,128,512]{4,3,2,1,0:T(8,128)(2,1)}, u32[]{:S(2)}) copy-start(bf16[3,3,3,128,512]{4,3,2,1,0:T(8,128)(2,1)} %param.18) | copy-start | bytes 10616836
  114.9 6.9 %copy-start.6 = (bf16[3,3,3,128,512]{4,3,2,1,0:T(8,128)(2,1)S(1)}, bf16[3,3,3,128,512]{4,3,2,1,0:T(8,128)(2,1)}, u32[]{:S(2)}) copy-start(bf16[3,3,3,128,512]{4,3,2,1,0:T(8,128)(2,1)} %param.19) | copy-start | bytes 10616836
Sparse Core Ops, SparseCore 0:
  8.9 22.3 all-gather.3
  32.8 34.4 all-gather.5
  68.9 22.5 all-gather.7
where the time goes:
time: 138 us
  blocking collectives  47.7 us (35%)
  waiting for transfers between devices  45.5 us (33%)
  matrix products  13.8 us (10%)
  between operations  13.6 us (10%)
  starting transfers between devices  9.45 us (7%)
  local copies, waits for them, and re-layouts  6.56 us (5%)
    psum x1, blocking collectives, attend(): lax.psum(state.astype(jnp.bfloat16), 'row').astype(jnp.float32)  21.4 us
    all_gather x1, waiting for transfers between devices, local(): lax.all_gather(qkv_weight, 'frame', axis=1, tiled=True)  12.1 us
    all_gather x1, waiting for transfers between devices, local(): lax.all_gather(in_weight, 'frame', axis=2, tiled=True)  10.4 us
    all_gather x1, waiting for transfers between devices, local(): lax.all_gather(down_weight, 'frame', axis=0, tiled=True)  9.69 us
    all_gather x1, blocking collectives, local(): lax.all_gather(out_weight, 'frame', axis=0, tiled=True)  8.65 us
    ppermute x2, waiting for transfers between devices, padded_2(): lax.ppermute(head, axis, [((i + 1) % count, i) for i in range(ends)])  8.23 us
    ppermute x2, starting transfers between devices, padded_2(): lax.ppermute(tail, axis, [(i, (i + 1) % count) for i in range(ends)])  6.78 us
    all_to_all x1, blocking collectives, local(): lax.all_to_all(final, 'frame', split_axis=2, concat_axis=3, tiled=True)  6.3 us
  transfers between devices with their start and end apart: 7, of which 7 were waited for; matrix products, arithmetic and copies ran while one was open for 8% of the time, Pallas kernels for 0%

commit v1 on v0

--- a/solution.py
+++ b/solution.py
@@ -4,6 +4,15 @@
 from jax.sharding import PartitionSpec as P
 
 HEAD = 32
+
+
+def search_the_local_data(t0, dim_k):
+    t0 = jnp.moveaxis(t0, 0, dim_k)
+    long_array = t0.shape
+    d_next = t0.reshape(
+        *long_array[:dim_k], long_array[dim_k] * long_array[dim_k + 1], *long_array[dim_k + 2 :]
+    )
+    return d_next
 
 
 def padded_2(cells, sides, width):
@@ -102,13 +111,36 @@
     conv_first,
     conv_second,
 ):
+
+    def attach_leaves(load, axis_name, in_dim, piece_in, d0):
+        arr_next = lax.axis_size(axis_name)
+        passed = lax.axis_index(axis_name)
+        y2, r_now, value_now = (arr_next, passed, load.shape[in_dim])
+        xs_all = [(j, (j + 1) % y2) for j in range(y2)]
+        vals = []
+        block_next = load
+        w = 0
+        while w < y2:
+            current_arr = block_next if w == y2 - 1 else lax.ppermute(block_next, axis_name, xs_all)
+            z2 = piece_in(block_next, (r_now - w) % y2 * value_now)
+            vals.append(z2)
+            block_next = current_arr
+            w += 1
+        plain = jnp.stack(vals, axis=0)
+        vals = plain[(r_now - jnp.arange(y2)) % y2]
+        upper = search_the_local_data(vals, d0)
+        return upper
+
     frames, height, columns, width = latent.shape
     place = lax.axis_index("frame")
-    packed = jnp.einsum(
-        "frwc,kjc->frwkj",
-        latent,
-        lax.all_gather(qkv_weight, "frame", axis=1, tiled=True),
-        preferred_element_type=jnp.float32,
+    packed = attach_leaves(
+        qkv_weight,
+        "frame",
+        1,
+        lambda own_block, offset: jnp.einsum(
+            "frwc,kjc->frwkj", latent, own_block, preferred_element_type=jnp.float32
+        ),
+        4,
     ).astype(jnp.bfloat16)
     mixed = attend(packed)
     section = mixed

time: 138 us -> 139 us (level)
  waiting for transfers between devices: 45.5 us -> 34.2 us
  blocking collectives: 47.7 us -> 58.4 us
    ppermute x0 -> x3, waiting for transfers between devices: none -> 22.5 us  [attach_leaves(): lax.ppermute(block_next, axis_name, xs_all)]
    all_gather x1 -> x0, waiting for transfers between devices: 12.1 us -> none  [local(): lax.all_gather(qkv_weight, 'frame', axis=1, tiled=True)]
    all_gather x1, waiting for transfers between devices: 10.4 us -> 0.02 us  [local(): lax.all_gather(in_weight, 'frame', axis=2, tiled=True)]
    all_gather x1, blocking collectives: 8.65 us -> 18.4 us  [local(): lax.all_gather(out_weight, 'frame', axis=0, tiled=True)]
    all_gather x1, waiting for transfers between devices: 9.69 us -> 0.02 us  [local(): lax.all_gather(down_weight, 'frame', axis=0, tiled=True)]
    ppermute x0 -> x3, starting transfers between devices: none -> 3.02 us  [attach_leaves(): lax.ppermute(block_next, axis_name, xs_all)]
    ppermute x2, starting transfers between devices: 6.78 us -> 5.08 us  [padded_2(): lax.ppermute(tail, axis, [(i, (i + 1) % count) for i in range(ends)])]
    unnamed x19 -> x21, local copies, waits for them, and re-layouts: 3.87 us -> 3.89 us
  transfers between devices with their start and end apart: 7 -> 9, of which waited for: 7 -> 6; matrix products, arithmetic and copies ran while one was open for 8% -> 6% of each run, Pallas kernels for 0% -> 0%
where the time goes in v1:
time: 139 us
  blocking collectives  58.4 us (42%)
  waiting for transfers between devices  34.2 us (25%)
  between operations  13.9 us (10%)
  matrix products  12.9 us (9%)
  starting transfers between devices  10.7 us (8%)
  local copies, waits for them, and re-layouts  7.18 us (5%)
    ppermute x3, waiting for transfers between devices, attach_leaves(): lax.ppermute(block_next, axis_name, xs_all)  22.5 us
    psum x1, blocking collectives, attend(): lax.psum(state.astype(jnp.bfloat16), 'row').astype(jnp.float32)  22.2 us
    all_gather x1, blocking collectives, local(): lax.all_gather(out_weight, 'frame', axis=0, tiled=True)  18.4 us
    ppermute x2, waiting for transfers between devices, padded_2(): lax.ppermute(head, axis, [((i + 1) % count, i) for i in range(ends)])  8.47 us
    all_to_all x1, blocking collectives, local(): lax.all_to_all(final, 'frame', split_axis=2, concat_axis=3, tiled=True)  6.42 us
    all_gather x1, blocking collectives, local(): joined = lax.all_gather(hidden_conv, 'frame', axis=3, tiled=True)  5.94 us
    dot_general x18, matrix products, conv_tile(): jnp.einsum('nci,coi->no', stacked.reshape(-1, 3, width), kernel[shift_tim...  5.74 us
    all_gather x1, blocking collectives, local(): gathered = lax.all_gather(second, 'frame', axis=0, tiled=True)  5.42 us
  transfers between devices with their start and end apart: 9, of which 6 were waited for; matrix products, arithmetic and copies ran while one was open for 6% of the time, Pallas kernels for 0%

profile of v1, /device:TPU:0, one launch (start us, length us, event | category | flops | bytes accessed | tf_op | source)
XLA Modules:
  0.0 138.7 jit_solution(11905137477514892311)
XLA Ops:
  6.5 2.4 %copy.34 = bf16[512,2,512]{2,0,1:T(8,128)(2,1)} copy(bf16[512,2,512]{2,1,0:T(2,128)(2,1)} %param.14) | data formatting | bytes 2097152 | tf_op args[4]
  9.0 0.5 collective-permute-start
  9.8 7.4 %collective-permute-done = bf16[3,128,512]{2,1,0:T(8,128)(2,1)S(1)} collective-permute-done((bf16[3,128,512]{2,1,0:T(8,128)(2,1)}, bf16[3,128,512]{2,1,0:T(8,128)(2,1)S(1)}, u32[]{:S(2)}, u32[]{:S(2)}) %collective-permute-start) | collective-permute-done | bytes 393248 | tf_op jit(solution)/shard_map/ppermute | solution.py:124
  17.3 18.4 %all_gather.15 = bf16[512,512]{1,0:T(8,128)(2,1)S(1)} all-gather(bf16[128,512]{1,0:T(8,128)(2,1)S(1)} %copy-done.3), channel_id=1, replica_groups=mesh['parts'=2,'row'=4,'frame'=4] {'frame'}, dimensions={0}, use_global_device_ids=true | all-gather | bytes 655360 | tf_op jit(solution)/shard_map/all_gather | solution.py:150
  35.6 2.4 %collective-permute-start.2 = (bf16[3,128,512]{2,1,0:T(8,128)(2,1)S(1)}, bf16[3,128,512]{2,1,0:T(8,128)(2,1)S(1)}, u32[]{:S(2)}, u32[]{:S(2)}) collective-permute-start(bf16[3,128,512]{2,1,0:T(8,128)(2,1)S(1)} %collective-permute-done.1), channel_id=1, source_target_pairs={{0,1},{1,2},{2,3},{3,0},{4,5},{5,6},{6,7},{7,4},{8,9},{9,10},{10,1... | collective-permute-start | bytes 1179656 | tf_op jit(solution)/shard_map/ppermute | solution.py:124
  38.8 15.0 %collective-permute-done.2 = bf16[3,128,512]{2,1,0:T(8,128)(2,1)S(1)} collective-permute-done((bf16[3,128,512]{2,1,0:T(8,128)(2,1)S(1)}, bf16[3,128,512]{2,1,0:T(8,128)(2,1)S(1)}, u32[]{:S(2)}, u32[]{:S(2)}) %collective-permute-start.2) | collective-permute-done | bytes 393248 | tf_op jit(solution)/shard_map/ppermute | solution.py:124
  54.2 0.6 gather_fusion
  55.5 22.2 %all-reduce.3 = (bf16[1,16,32,32]{3,2,1,0:T(8,128)(2,1)S(1)}, bf16[1,16,32]{2,1,0:T(8,128)(2,1)S(1)}) all-reduce(bf16[1,16,32,32]{3,2,1,0:T(8,128)(2,1)S(1)} %fusion.5, bf16[1,16,32]{2,1,0:T(8,128)(2,1)S(1)} %bitcast.400), channel_id=1, replica_groups=mesh['parts'=2,'row'=4,'frame'=4] {'row'}, use_global_device_ids=true, to_apply=%region_0.1 | all-reduce | flops 16896 | bytes 67584 | tf_op jit(solution)/shard_map/psum | solution.py:50
  79.4 3.1 %multiply_convert_fusion = bf16[2,16,2,2048]{3,1,2,0:T(8,128)(2,1)S(1)} fusion(bf16[512,2,2048]{2,0,1:T(8,128)(2,1)} %all-gather.3.cloned.1.call-done, bf16[1,2,16,512]{3,2,1,0:T(8,128)(2,1)S(1)} %fusion.183), kind=kOutput, calls=%fused_computation.156 | convolution fusion | flops 134873088 | bytes 4489216 | tf_op jit(solution)/shard_map/frwc,ckj->frwkj/dot_general | solution.py:155
  82.5 1.3 collective-permute-start.3
  83.8 1.3 collective-permute-start.4
  85.2 1.2 collective-permute-done.3
  86.3 4.4 %collective-permute-done.4 = bf16[1,1,16,2,2048]{4,2,3,1,0:T(8,128)(2,1)S(1)} collective-permute-done((bf16[1,1,16,2,2048]{4,2,3,1,0:T(8,128)(2,1)S(1)}, bf16[1,1,16,2,2048]{4,2,3,1,0:T(8,128)(2,1)S(1)}, u32[]{:S(2)}, u32[]{:S(2)}) %collective-permute-start.4) | collective-permute-done | bytes 131104 | tf_op jit(solution)/shard_map/ppermute | solution.py:28
  91.5 2.1 %multiply_reduce_fusion = (f32[2,16]{1,0:T(2,128)S(1)}, f32[2,16,512]{2,1,0:T(8,128)S(1)}) fusion(bf16[2048,512]{1,0:T(8,128)(2,1)} %all-gather.5.cloned.1.call-done, f32[1,2,16,2,2048]{4,2,3,1,0:T(8,128)S(1)} %fusion.77), kind=kOutput, calls=%fused_computation.272 | convolution fusion | flops 67534816 | bytes 2687104 | tf_op jit(solution)/shard_map/frwj,jc->frwc/dot_general | solution.py:164
  93.7 5.4 %all_gather.18 = bf16[4,2,16,512]{3,2,1,0:T(8,128)(2,1)S(1)} all-gather(bf16[1,2,16,512]{3,2,1,0:T(8,128)(2,1)S(1)} %fusion.182), channel_id=1, replica_groups=mesh['parts'=2,'row'=4,'frame'=4] {'frame'}, dimensions={0}, use_global_device_ids=true | all-gather | bytes 163840 | tf_op jit(solution)/shard_map/all_gather | solution.py:171
  99.1 3.8 %collective-permute-start.5 = (bf16[4,2,16,512]{3,2,1,0:T(8,128)(2,1)S(1)}, bf16[4,2,16,512]{3,2,1,0:T(8,128)(2,1)S(1)}, u32[]{:S(2)}, u32[]{:S(2)}) collective-permute-start(bf16[4,2,16,512]{3,2,1,0:T(8,128)(2,1)S(1)} %all_gather.18), channel_id=1, source_target_pairs={{0,4},{4,8},{8,12},{1,5},{5,9},{9,13},{2,6},{6,10},{10,14},{3,7},{... | collective-permute-start | bytes 393224 | tf_op jit(solution)/shard_map/ppermute | solution.py:26
  102.9 1.3 collective-permute-start.6
  104.2 1.9 %collective-permute-done.5 = bf16[4,2,16,512]{3,2,1,0:T(8,128)(2,1)S(1)} collective-permute-done((bf16[4,2,16,512]{3,2,1,0:T(8,128)(2,1)S(1)}, bf16[4,2,16,512]{3,2,1,0:T(8,128)(2,1)S(1)}, u32[]{:S(2)}, u32[]{:S(2)}) %collective-permute-start.5) | collective-permute-done | bytes 131104 | tf_op jit(solution)/shard_map/ppermute | solution.py:26
  106.1 4.1 %collective-permute-done.6 = bf16[4,2,16,512]{3,2,1,0:T(8,128)(2,1)S(1)} collective-permute-done((bf16[4,2,16,512]{3,2,1,0:T(8,128)(2,1)S(1)}, bf16[4,2,16,512]{3,2,1,0:T(8,128)(2,1)S(1)}, u32[]{:S(2)}, u32[]{:S(2)}) %collective-permute-start.6) | collective-permute-done | bytes 131104 | tf_op jit(solution)/shard_map/ppermute | solution.py:28
  110.3 0.8 pad_slice_fusion.23
  111.2 1.0 copy-done.6
  115.8 5.9 %all_gather.19 = bf16[4,4,16,512]{3,2,1,0:T(8,128)(2,1)S(1)} all-gather(bf16[4,4,16,128]{3,2,1,0:T(8,128)(2,1)S(1)} %multiply_convert_fusion.1), channel_id=1, replica_groups=mesh['parts'=2,'row'=4,'frame'=4] {'frame'}, dimensions={3}, use_global_device_ids=true | all-gather | bytes 327680 | tf_op jit(solution)/shard_map/all_gather | solution.py:178
  124.8 6.4 %all_to_all.18 = bf16[4,2,16,128]{3,1,0,2:T(2,128)(2,1)S(1)} all-to-all(bf16[4,2,16,128]{3,1,0,2:T(2,128)(2,1)S(1)} %copy.36), channel_id=1, replica_groups=mesh['parts'=2,'row'=4,'frame'=4] {'frame'}, dimensions={2} | all-to-all | bytes 65536 | tf_op jit(solution)/shard_map/all_to_all | solution.py:182
  131.2 0.6 all_to_all.16
  (82 shorter events, 11.1 us)
Async XLA Ops:
  6.5 31.5 %copy-start.1 = (bf16[3,128,512]{2,1,0:T(8,128)(2,1)S(1)}, bf16[3,128,512]{2,1,0:T(8,128)(2,1)}, u32[]{:S(2)}) copy-start(bf16[3,128,512]{2,1,0:T(8,128)(2,1)} %param.11) | copy-start | bytes 1179652
  6.5 10.7 %copy-start.3 = (bf16[128,512]{1,0:T(8,128)(2,1)S(1)}, bf16[128,512]{1,0:T(8,128)(2,1)}, u32[]{:S(2)}) copy-start(bf16[128,512]{1,0:T(8,128)(2,1)} %param.12) | copy-start | bytes 393220
  6.5 31.5 %copy-start = (bf16[1,2,16,512]{3,2,1,0:T(8,128)(2,1)S(1)}, bf16[1,2,16,512]{3,2,1,0:T(8,128)(2,1)}, u32[]{:S(2)}) copy-start(bf16[1,2,16,512]{3,2,1,0:T(8,128)(2,1)} %param.10) | copy-start | bytes 98308
  6.5 72.8 %all-gather.3.cloned.1.call-start = ((), (), s32[]{:S(2)}) async-start(), calls=%async_computation.1 | async-start | bytes 5242880 | tf_op jit(solution)/shard_map/all_gather | solution.py:158
  9.0 82.4 %all-gather.5.cloned.1.call-start = ((), (), s32[]{:S(2)}) async-start(), calls=%async_computation.2 | async-start | bytes 2621440 | tf_op jit(solution)/shard_map/all_gather | solution.py:167
  9.0 8.1 %collective-permute-start = (bf16[3,128,512]{2,1,0:T(8,128)(2,1)}, bf16[3,128,512]{2,1,0:T(8,128)(2,1)S(1)}, u32[]{:S(2)}, u32[]{:S(2)}) collective-permute-start(bf16[3,128,512]{2,1,0:T(8,128)(2,1)} %param.11), channel_id=1, source_target_pairs={{0,1},{1,2},{2,3},{3,0},{4,5},{5,6},{6,7},{7,4},{8,9},{9,10},{10,1... | collective-permute-start | bytes 1179656 | tf_op jit(solution)/shard_map/ppermute | solution.py:124
  17.2 18.5 %collective-permute-start.1 = (bf16[3,128,512]{2,1,0:T(8,128)(2,1)S(1)}, bf16[3,128,512]{2,1,0:T(8,128)(2,1)S(1)}, u32[]{:S(2)}, u32[]{:S(2)}) collective-permute-start(bf16[3,128,512]{2,1,0:T(8,128)(2,1)S(1)} %collective-permute-done), channel_id=1, source_target_pairs={{0,1},{1,2},{2,3},{3,0},{4,5},{5,6},{6,7},{7,4},{8,9},{9,10},{10,1... | collective-permute-start | bytes 1179656 | tf_op jit(solution)/shard_map/ppermute | solution.py:124
  35.6 18.2 %collective-permute-start.2 = (bf16[3,128,512]{2,1,0:T(8,128)(2,1)S(1)}, bf16[3,128,512]{2,1,0:T(8,128)(2,1)S(1)}, u32[]{:S(2)}, u32[]{:S(2)}) collective-permute-start(bf16[3,128,512]{2,1,0:T(8,128)(2,1)S(1)} %collective-permute-done.1), channel_id=1, source_target_pairs={{0,1},{1,2},{2,3},{3,0},{4,5},{5,6},{6,7},{7,4},{8,9},{9,10},{10,1... | collective-permute-start | bytes 1179656 | tf_op jit(solution)/shard_map/ppermute | solution.py:124
  38.3 40.9 %copy-start.4 = (f32[512]{0:T(512)S(1)}, f32[512]{0:T(512)}, u32[]{:S(2)}) copy-start(f32[512]{0:T(512)} %param.13) | copy-start | bytes 6148
  79.3 5.8 %copy-start.2 = (f32[3,3,2,2048]{3,2,1,0:T(2,128)S(1)}, f32[3,3,2,2048]{3,2,1,0:T(2,128)}, u32[]{:S(2)}) copy-start(f32[3,3,2,2048]{3,2,1,0:T(2,128)} %param.15) | copy-start | bytes 442372
  82.5 3.8 %collective-permute-start.3 = (bf16[1,1,16,2,2048]{4,2,3,1,0:T(8,128)(2,1)S(1)}, bf16[1,1,16,2,2048]{4,2,3,1,0:T(8,128)(2,1)S(1)}, u32[]{:S(2)}, u32[]{:S(2)}) collective-permute-start(bf16[1,1,16,2,2048]{4,2,3,1,0:T(8,128)(2,1)S(1)} %get-tuple-element.62), channel_id=1, source_target_pairs={{0,4},{4,8},{8,12},{1,5},{5,9},{9,13},{2,6},{6,10},{10,14},{3,7},{... | collective-permute-start | bytes 393224 | tf_op jit(solution)/shard_map/ppermute | solution.py:26
  83.8 6.9 %collective-permute-start.4 = (bf16[1,1,16,2,2048]{4,2,3,1,0:T(8,128)(2,1)S(1)}, bf16[1,1,16,2,2048]{4,2,3,1,0:T(8,128)(2,1)S(1)}, u32[]{:S(2)}, u32[]{:S(2)}) collective-permute-start(bf16[1,1,16,2,2048]{4,2,3,1,0:T(8,128)(2,1)S(1)} %get-tuple-element.63), channel_id=1, source_target_pairs={{4,0},{8,4},{12,8},{5,1},{9,5},{13,9},{6,2},{10,6},{14,10},{7,3},{... | collective-permute-start | bytes 393224 | tf_op jit(solution)/shard_map/ppermute | solution.py:28
  85.2 8.4 %copy-start.5 = (f32[512]{0:T(512)S(1)}, f32[512]{0:T(512)}, u32[]{:S(2)}) copy-start(f32[512]{0:T(512)} %param.17) | copy-start | bytes 6148
  99.1 7.0 %collective-permute-start.5 = (bf16[4,2,16,512]{3,2,1,0:T(8,128)(2,1)S(1)}, bf16[4,2,16,512]{3,2,1,0:T(8,128)(2,1)S(1)}, u32[]{:S(2)}, u32[]{:S(2)}) collective-permute-start(bf16[4,2,16,512]{3,2,1,0:T(8,128)(2,1)S(1)} %all_gather.18), channel_id=1, source_target_pairs={{0,4},{4,8},{8,12},{1,5},{5,9},{9,13},{2,6},{6,10},{10,14},{3,7},{... | collective-permute-start | bytes 393224 | tf_op jit(solution)/shard_map/ppermute | solution.py:26
  102.9 7.4 %collective-permute-start.6 = (bf16[4,2,16,512]{3,2,1,0:T(8,128)(2,1)S(1)}, bf16[4,2,16,512]{3,2,1,0:T(8,128)(2,1)S(1)}, u32[]{:S(2)}, u32[]{:S(2)}) collective-permute-start(bf16[4,2,16,512]{3,2,1,0:T(8,128)(2,1)S(1)} %all_gather.18), channel_id=1, source_target_pairs={{4,0},{8,4},{12,8},{5,1},{9,5},{13,9},{6,2},{10,6},{14,10},{7,3},{... | collective-permute-start | bytes 393224 | tf_op jit(solution)/shard_map/ppermute | solution.py:28
  110.3 2.0 %copy-start.6 = (bf16[3,3,3,128,512]{4,3,2,1,0:T(8,128)(2,1)S(1)}, bf16[3,3,3,128,512]{4,3,2,1,0:T(8,128)(2,1)}, u32[]{:S(2)}) copy-start(bf16[3,3,3,128,512]{4,3,2,1,0:T(8,128)(2,1)} %param.18) | copy-start | bytes 10616836
  115.3 6.9 %copy-start.7 = (bf16[3,3,3,128,512]{4,3,2,1,0:T(8,128)(2,1)S(1)}, bf16[3,3,3,128,512]{4,3,2,1,0:T(8,128)(2,1)}, u32[]{:S(2)}) copy-start(bf16[3,3,3,128,512]{4,3,2,1,0:T(8,128)(2,1)} %param.19) | copy-start | bytes 10616836
Sparse Core Ops, SparseCore 0:
  9.1 45.7 all-gather.2
  56.4 24.7 all-gather.4
